TPU v7x, 512 devices: a whole 4x4x16 slice. The times are simulated.
512 devices in a mesh: tile: 32 (over z, core), chan: 16 (over y, x).
Axes of the slice: x: 4, y: 4, z: 16, core: 2. Of those that a mesh axis runs over, the one named last changes fastest.
Arguments:
- fields: float32 [64, 1024, 411], P('chan', 'tile'), may hold values from -12 to 12
- diffusivity: float32 [64, 1024], P('chan', 'tile'), may hold values from 0.02 to 0.24
- owners: int32 [4096, 1], replicated, may hold values from 0 to 31; in each aligned block of 128 rows (0 to 127, 128 to 255, ...) at most 8 rows name the same one
- observed: bfloat16 [8192, 6144], P('tile', 'chan'), may hold values from -6 to 6
- usable: int32 [8192], P('tile'), may hold values 0 or 1
- w_hidden: bfloat16 [411, 2048], P(None, 'chan'), may hold values from -0.3125 to 0.3125
- b_hidden: float32 [2048], P('chan'), may hold values from -3 to 3
- w_radiance: bfloat16 [2048, 6144], P(None, 'chan'), may hold values from -0.125 to 0.125
- b_radiance: float32 [6144], P('chan'), may hold values from -3 to 3
- inv_cov: bfloat16 [6144, 6144], P('tile', 'chan'), may hold values from -6 to 22
Outputs:
- gradient: float32 [64, 1024, 411], P('chan', 'tile')
Inputs may be any that keep to these rules, and one draw needn't show every extreme that they name: `owners`: in each tile's block of 128 consecutive entries no owner appears more than 8 times, and in some blocks one appears exactly 8 times.
All inputs are finite; a program needn't handle non-finite values. No bound on the sum of `usable` on one device may be relied on, other than what follows from the above.
Results may differ from a plain program's by a relative error of at most 0.0045.
Values may be sent and summed in bfloat16 or wider, within the bound.
A program may use at most 64 MiB of HBM per device.

v0:
```python
import jax
import jax.numpy as jnp
from jax import lax
from jax.sharding import PartitionSpec as P


def padded_2(value, sides, width, wrap):
    for axis, dim in sides:
        devices, length = (lax.axis_size(axis), value.shape[dim])
        up = [(i, (i + 1) % devices) for i in range(devices if wrap else devices - 1)]
        down = [(j, i) for i, j in up]
        last = lax.slice_in_dim(value, length - width, length, axis=dim)
        first = lax.slice_in_dim(value, 0, width, axis=dim)
        before = lax.ppermute(last, axis, up)
        after = lax.ppermute(first, axis, down)
        value = jnp.concatenate([before, value, after], axis=dim)
    return value


def add_rims(values):
    rowwise = padded_2(values, (("chan", 0),), 1, False)
    return padded_2(rowwise, (("tile", 1),), 1, True)


def body(
    fields,
    diffusivity,
    owners,
    observed,
    usable,
    w_hidden,
    b_hidden,
    w_radiance,
    b_radiance,
    inv_cov,
):
    tile_count = lax.axis_size("tile")
    chan_count = lax.axis_size("chan")
    tile_index = lax.axis_index("tile")
    chan_index = lax.axis_index("chan")
    slot_count = observed.shape[0]
    capacity = slot_count // tile_count
    cells_across, cells_along, features = fields.shape
    own_cols = cells_across // 4 * (cells_along // 4)
    tile_cols = chan_count * own_cols
    hidden_dev = w_hidden.shape[1]
    owner_table = owners[:, 0].reshape(tile_count, tile_cols)
    owner_hits = (
        owner_table[:, :, None] == jnp.arange(tile_count, dtype=jnp.int32)[None, None, :]
    ).astype(jnp.int32)
    before = jnp.sum((jnp.cumsum(owner_hits, axis=1) - owner_hits) * owner_hits, axis=2)
    tallies = jnp.sum(owner_hits, axis=1)
    slot_of = lax.dynamic_index_in_dim(
        owner_table * capacity + before, tile_index, 0, keepdims=False
    )
    arriving = lax.dynamic_index_in_dim(tallies, tile_index, 1, keepdims=False)
    occupied = (jnp.arange(capacity, dtype=jnp.int32)[None, :] < arriving[:, None]).reshape(
        slot_count
    )
    grouped = fields.reshape(cells_across // 4, 4, cells_along // 4, 4, features)
    columns = (
        (jnp.sum(grouped, axis=(1, 3)) * 0.0625).reshape(own_cols, features).astype(jnp.bfloat16)
    )
    placer = (slot_of[None, :] == jnp.arange(slot_count, dtype=jnp.int32)[:, None]).astype(
        jnp.bfloat16
    )
    picks = placer
    outgoing = jnp.dot(
        picks,
        lax.all_gather(columns, "chan", axis=0, tiled=True),
        preferred_element_type=jnp.float32,
    )
    incoming = lax.all_to_all(
        outgoing.astype(jnp.bfloat16), "tile", split_axis=0, concat_axis=0, tiled=True
    )
    preact = lax.dot_general(
        w_hidden, incoming, (((0,), (1,)), ((), ())), preferred_element_type=jnp.float32
    )
    preact = preact + b_hidden[:, None]
    squash = jax.nn.sigmoid(preact)
    active = (preact * squash).astype(jnp.bfloat16)
    weights = w_radiance
    radiance = lax.dot_general(
        lax.all_gather(active, "chan", axis=0, tiled=True),
        weights,
        (((0,), (0,)), ((), ())),
        preferred_element_type=jnp.float32,
    )
    radiance = radiance + b_radiance[None, :]
    in_use = usable.astype(jnp.float32) * occupied.astype(jnp.float32)
    departure = ((radiance - observed.astype(jnp.float32)) * in_use[:, None]).astype(jnp.bfloat16)
    all_depart = lax.all_gather(departure, "chan", axis=1, tiled=True)
    picks = all_depart
    cotangent = jnp.dot(
        picks,
        lax.all_gather(inv_cov, "tile", axis=0, tiled=True),
        preferred_element_type=jnp.float32,
    )
    cotangent = cotangent.astype(jnp.bfloat16)
    weights = w_radiance
    full_sum = lax.psum(
        lax.dot_general(
            weights, cotangent, (((1,), (1,)), ((), ())), preferred_element_type=jnp.float32
        ),
        "chan",
    )
    grad_hidden = lax.dynamic_slice_in_dim(full_sum, chan_index * hidden_dev, hidden_dev, 0)
    slope_term = squash * (1.0 + preact * (1.0 - squash))
    grad_pre = (grad_hidden * slope_term).astype(jnp.bfloat16)
    part_grad = lax.dot_general(
        grad_pre, w_hidden, (((0,), (1,)), ((), ())), preferred_element_type=jnp.float32
    )
    summed_grad = lax.psum(part_grad, "chan")
    returned = lax.all_to_all(summed_grad, "tile", split_axis=0, concat_axis=0, tiled=True)
    own_slots = lax.dynamic_slice_in_dim(slot_of, chan_index * own_cols, own_cols, 0)
    column_grad = jnp.take(returned, own_slots, axis=0)
    spread = jnp.repeat(
        column_grad.reshape(cells_across // 4, cells_along // 4, features), 4, axis=0
    )
    adjoint = jnp.repeat(spread, 4, axis=1) * 0.0625
    kappa_root = jnp.sqrt(diffusivity)
    root_rim = add_rims(kappa_root)
    coef_north = (kappa_root * root_rim[2:, 1:-1])[:, :, None]
    coef_south = (kappa_root * root_rim[:-2, 1:-1])[:, :, None]
    coef_east = (kappa_root * root_rim[1:-1, 2:])[:, :, None]
    coef_west = (kappa_root * root_rim[1:-1, :-2])[:, :, None]
    for sweep_index in range(2):
        padded = add_rims(adjoint)
        adjoint = (
            adjoint
            + coef_north * (padded[2:, 1:-1] - adjoint)
            + coef_south * (padded[:-2, 1:-1] - adjoint)
            + coef_east * (padded[1:-1, 2:] - adjoint)
            + coef_west * (padded[1:-1, :-2] - adjoint)
        )
    return adjoint


def solution(mesh):
    placed = (
        P("chan", "tile", None),
        P("chan", "tile"),
        P(),
        P("tile", "chan"),
        P("tile"),
        P(None, "chan"),
        P("chan"),
        P(None, "chan"),
        P("chan"),
        P("tile", "chan"),
    )
    return jax.shard_map(
        body, mesh=mesh, in_specs=placed, out_specs=P("chan", "tile", None), check_vma=False
    )
```

profile of v0, /device:TPU:6, one launch (start us, length us, event | category | flops | bytes accessed | tf_op | source)
XLA Modules:
  0.0 599.1 jit_solution(5220718163068988109)
XLA Ops:
  6.6 0.9 copy.26
  7.5 1.0 reduce_sum.35
  8.6 3.3 convert_reduce_fusion
  12.0 26.5 %all_gather.12 = bf16[128,411]{1,0:T(8,128)(2,1)S(1)} all-gather(bf16[8,411]{1,0:T(8,128)(2,1)S(1)} %multiply_convert_fusion.3), channel_id=1, replica_groups=mesh['tile'=32,'chan'=16] {'chan'}, dimensions={0}, use_global_device_ids=true | all-gather | bytes 111792 | tf_op jit(solution)/shard_map/all_gather | solution.py:70
  38.5 0.2 dynamic-slice_reduce_fusion
  38.6 0.3 convolution_convert_fusion
  38.9 0.1 copy.29
  39.1 35.1 %all_to_all.24 = bf16[32,8,411]{2,1,0:T(8,128)(2,1)S(1)} all-to-all(bf16[32,8,411]{2,1,0:T(8,128)(2,1)S(1)} %bitcast.26), channel_id=1, replica_groups=mesh['tile'=32,'chan'=16] {'tile'}, dimensions={0} | all-to-all | bytes 420864 | tf_op jit(solution)/shard_map/all_to_all | solution.py:73
  74.2 0.9 multiply_convert_fusion.1
  75.2 0.2 dynamic-slice_reduce_fusion.1
  75.3 0.1 iota_compare_fusion.4
  75.4 0.1 lt.53
  75.5 47.4 %all-gather.4.cloned.1.call-done = bf16[2048,256]{0,1:T(8,128)(2,1)} async-done(((bf16[128,256]{0,1:T(8,128)(2,1)}), bf16[2048,256]{0,1:T(8,128)(2,1)}) %all-gather.4.cloned.1.call-update) | async-done | bytes 1048592 | tf_op jit(solution)/shard_map/all_gather | solution.py:84
  122.9 2.6 fusion.6
  125.6 0.7 all-gather.8.cloned.1.call-update
  126.3 66.2 %all-gather.6.cloned.1.call-done = bf16[256,6144]{1,0:T(8,128)(2,1)} async-done(((bf16[256,384]{1,0:T(8,128)(2,1)}), bf16[256,6144]{1,0:T(8,128)(2,1)}) %all-gather.6.cloned.1.call-update) | async-done | bytes 3145744 | tf_op jit(solution)/shard_map/all_gather | solution.py:92
  192.5 75.9 %all-gather.8.cloned.1.call-done = bf16[6144,384]{1,0:T(8,128)(2,1)} async-done(((bf16[192,384]{1,0:T(8,128)(2,1)}), bf16[6144,384]{1,0:T(8,128)(2,1)}) %all-gather.8.cloned.1.call-update) | async-done | bytes 4718608 | tf_op jit(solution)/shard_map/all_gather | solution.py:96
  268.4 7.1 %convolution_bitcast_fusion = f32[2048,256]{0,1:T(8,128)} fusion(bf16[2048,384]{1,0:T(8,128)(2,1)S(1)} %copy-done, bf16[256,6144]{1,0:T(8,128)(2,1)} %all-gather.6.cloned.1.call-done, bf16[6144,384]{1,0:T(8,128)(2,1)} %all-gather.8.cloned.1.call-done), kind=kOutput, calls=%fused_computation.5 | convolution fusion | flops 1610711040 | bytes 11534336 | tf_op jit(solution)/shard_map/dot_general | solution.py:102
  275.6 118.8 %all-reduce.3.cloned.1.call-done = f32[2048,256]{0,1:T(8,128)} async-done(((f32[2048,256]{0,1:T(8,128)}), f32[2048,256]{0,1:T(8,128)}) %all-reduce.3.cloned.1.call-update) | async-done | bytes 2097168 | tf_op jit(solution)/shard_map/psum | solution.py:101
  394.4 2.0 convolution_bitcast_fusion.1
  396.3 117.1 %all-reduce.5.cloned.1.call-done = f32[32,8,411]{2,1,0:T(8,128)} async-done(((f32[32,8,411]{2,1,0:T(8,128)}), f32[32,8,411]{2,1,0:T(8,128)}) %all-reduce.5.cloned.1.call-update) | async-done | bytes 420880 | tf_op jit(solution)/shard_map/psum | solution.py:113
  513.4 12.6 %all-to-all-start.1 = ((f32[32,8,411]{2,1,0:T(8,128)}), f32[32,8,411]{2,1,0:T(8,128)S(1)}, u32[]{:S(2)}, u32[]{:S(2)}) async-start(f32[32,8,411]{2,1,0:T(8,128)} %all-reduce.5.cloned.1.call-done), calls=%async_computation.1 | async-start | bytes 1048576 | tf_op jit(solution)/shard_map/all_to_all | solution.py:114
  526.1 3.4 collective-permute-start.2
  529.4 2.5 collective-permute-start
  531.9 0.2 dynamic-slice_reduce_fusion.2
  532.2 4.8 collective-permute-done
  537.0 0.1 fusion.40
  537.1 1.7 collective-permute-start.4
  538.8 21.3 %all-to-all-done.1 = f32[32,8,411]{2,1,0:T(8,128)S(1)} async-done(((f32[32,8,411]{2,1,0:T(8,128)}), f32[32,8,411]{2,1,0:T(8,128)S(1)}, u32[]{:S(2)}, u32[]{:S(2)}) %all-to-all-start.1) | async-done | bytes 420896 | tf_op jit(solution)/shard_map/all_to_all | solution.py:114
  560.0 0.6 gather_fusion
  560.6 0.1 select_multiply_fusion
  560.7 3.4 collective-permute-start.3
  564.1 2.5 collective-permute-start.1
  566.6 0.1 pad_maximum_fusion.25
  566.7 0.2 collective-permute-done.3
  566.9 5.5 collective-permute-done.1
  572.5 0.5 collective-permute-start.7
  573.0 0.8 collective-permute-done.5
  573.9 2.9 collective-permute-done.7
  576.8 0.2 fusion.23
  577.0 1.9 collective-permute-start.9
  579.0 3.9 collective-permute-start.8
  582.9 0.3 collective-permute-done.9
  583.2 4.0 collective-permute-done.8
  587.3 0.5 collective-permute-start.11
  587.8 0.9 collective-permute-done.10
  588.7 2.9 collective-permute-done.11
  591.6 0.9 fusion.11
  (49 shorter events, 0.7 us)
Async XLA Ops:
  6.5 116.4 %copy-start = (bf16[2048,384]{1,0:T(8,128)(2,1)S(1)}, bf16[2048,384]{1,0:T(8,128)(2,1)}, u32[]{:S(2)}) copy-start(bf16[2048,384]{1,0:T(8,128)(2,1)} %param.17) | copy-start | bytes 4718596
  6.5 67.7 %copy-start.1 = (bf16[411,128]{1,0:T(8,128)(2,1)S(1)}, bf16[411,128]{1,0:T(8,128)(2,1)}, u32[]{:S(2)}) copy-start(bf16[411,128]{1,0:T(8,128)(2,1)} %param.15) | copy-start | bytes 315652
  6.5 67.7 %copy-start.6 = (f32[128]{0:T(128)S(1)}, f32[128]{0:T(128)}, u32[]{:S(2)}) copy-start(f32[128]{0:T(128)} %param.16) | copy-start | bytes 1540
  6.5 69.0 %copy-start.3 = (s32[256]{0:T(256)S(1)}, s32[256]{0:T(256)}, u32[]{:S(2)}) copy-start(s32[256]{0:T(256)} %param.14) | copy-start | bytes 3076
  6.5 116.4 %copy-start.5 = (f32[384]{0:T(512)S(1)}, f32[384]{0:T(512)}, u32[]{:S(2)}) copy-start(f32[384]{0:T(512)} %param.18) | copy-start | bytes 4612
  6.5 116.4 %copy-start.4 = (bf16[256,384]{1,0:T(8,128)(2,1)S(1)}, bf16[256,384]{1,0:T(8,128)(2,1)}, u32[]{:S(2)}) copy-start(bf16[256,384]{1,0:T(8,128)(2,1)} %param.13) | copy-start | bytes 589828
  6.6 116.4 %all-gather.4.cloned.1.call-start = ((), (), s32[]{:S(2)}) async-start(), calls=%async_computation.2 | async-start | bytes 1114112 | tf_op jit(solution)/shard_map/all_gather | solution.py:84
  75.1 117.4 %all-gather.6.cloned.1.call-start = ((), (), s32[]{:S(2)}) async-start(), calls=%async_computation.3 | async-start | bytes 3342336 | tf_op jit(solution)/shard_map/all_gather | solution.py:92
  125.6 142.8 %all-gather.8.cloned.1.call-start = ((), (), s32[]{:S(2)}) async-start(), calls=%async_computation.4 | async-start | bytes 4866048 | tf_op jit(solution)/shard_map/all_gather | solution.py:96
  126.3 268.1 %all-reduce.3.cloned.1.call-start = ((), (), s32[]{:S(2)}) async-start(), calls=%async_computation.5 | async-start | bytes 4194304 | tf_op jit(solution)/shard_map/psum | solution.py:101
  275.5 250.5 %copy-start.2 = (f32[4,32]{1,0:T(4,128)S(1)}, f32[4,32]{1,0:T(4,128)}, u32[]{:S(2)}) copy-start(f32[4,32]{1,0:T(4,128)} %param.11) | copy-start | bytes 1540
  275.5 237.9 %all-reduce.5.cloned.1.call-start = ((), (), s32[]{:S(2)}) async-start(), calls=%async_computation.6 | async-start | bytes 1048576 | tf_op jit(solution)/shard_map/psum | solution.py:113
  513.4 46.6 %all-to-all-start.1 = ((f32[32,8,411]{2,1,0:T(8,128)}), f32[32,8,411]{2,1,0:T(8,128)S(1)}, u32[]{:S(2)}, u32[]{:S(2)}) async-start(f32[32,8,411]{2,1,0:T(8,128)} %all-reduce.5.cloned.1.call-done), calls=%async_computation.1 | async-start | bytes 1048576 | tf_op jit(solution)/shard_map/all_to_all | solution.py:114
  526.1 6.1 %collective-permute-start.2 = (f32[1,32]{1,0:T(1,128)S(1)}, f32[1,32]{1,0:T(1,128)S(1)}, u32[]{:S(2)}, u32[]{:S(2)}) collective-permute-start(f32[1,32]{1,0:T(1,128)S(1)} %get-tuple-element.23), channel_id=1, source_target_pairs={{0,1},{1,2},{2,3},{3,4},{4,5},{5,6},{6,7},{7,8},{8,9},{9,10},{10,1... | collective-permute-start | bytes 392 | tf_op jit(solution)/shard_map/ppermute | solution.py:14
  529.4 7.6 %collective-permute-start = (f32[1,32]{1,0:T(1,128)S(1)}, f32[1,32]{1,0:T(1,128)S(1)}, u32[]{:S(2)}, u32[]{:S(2)}) collective-permute-start(f32[1,32]{1,0:T(1,128)S(1)} %get-tuple-element.24), channel_id=1, source_target_pairs={{1,0},{2,1},{3,2},{4,3},{5,4},{6,5},{7,6},{8,7},{9,8},{10,9},{11,1... | collective-permute-start | bytes 392 | tf_op jit(solution)/shard_map/ppermute | solution.py:15
  537.1 29.5 %collective-permute-start.4 = (f32[6,1]{1,0:T(8,128)S(1)}, f32[6,1]{1,0:T(8,128)S(1)}, u32[]{:S(2)}, u32[]{:S(2)}) collective-permute-start(f32[6,1]{1,0:T(8,128)S(1)} %get-tuple-element.13), channel_id=1, source_target_pairs={{16,0},{32,16},{48,32},{64,48},{80,64},{96,80},{112,96},{128,112},... | collective-permute-start | bytes 80 | tf_op jit(solution)/shard_map/ppermute | solution.py:15
  538.8 27.8 %collective-permute-start.6 = (f32[6,1]{1,0:T(8,128)S(1)}, f32[6,1]{1,0:T(8,128)S(1)}, u32[]{:S(2)}, u32[]{:S(2)}) collective-permute-start(f32[6,1]{1,0:T(8,128)S(1)} %get-tuple-element.14), channel_id=1, source_target_pairs={{0,16},{16,32},{32,48},{48,64},{64,80},{80,96},{96,112},{112,128},... | collective-permute-start | bytes 80 | tf_op jit(solution)/shard_map/ppermute | solution.py:14
  560.7 6.2 %collective-permute-start.3 = (f32[1,32,411]{2,1,0:T(8,128)S(1)}, f32[1,32,411]{2,1,0:T(8,128)S(1)}, u32[]{:S(2)}, u32[]{:S(2)}) collective-permute-start(f32[1,32,411]{2,1,0:T(8,128)S(1)} %mul.151), channel_id=1, source_target_pairs={{0,1},{1,2},{2,3},{3,4},{4,5},{5,6},{6,7},{7,8},{8,9},{9,10},{10,1... | collective-permute-start | bytes 157832 | tf_op jit(solution)/shard_map/ppermute | solution.py:14
  564.1 8.3 %collective-permute-start.1 = (f32[1,32,411]{2,1,0:T(8,128)S(1)}, f32[1,32,411]{2,1,0:T(8,128)S(1)}, u32[]{:S(2)}, u32[]{:S(2)}) collective-permute-start(f32[1,32,411]{2,1,0:T(8,128)S(1)} %mul.151), channel_id=1, source_target_pairs={{1,0},{2,1},{3,2},{4,3},{5,4},{6,5},{7,6},{8,7},{9,8},{10,9},{11,1... | collective-permute-start | bytes 157832 | tf_op jit(solution)/shard_map/ppermute | solution.py:15
  572.4 1.4 collective-permute-start.5
  572.5 4.3 collective-permute-start.7
  577.0 6.2 %collective-permute-start.9 = (f32[1,32,411]{2,1,0:T(8,128)S(1)}, f32[1,32,411]{2,1,0:T(8,128)S(1)}, u32[]{:S(2)}, u32[]{:S(2)}) collective-permute-start(f32[1,32,411]{2,1,0:T(8,128)S(1)} %get-tuple-element.11), channel_id=1, source_target_pairs={{0,1},{1,2},{2,3},{3,4},{4,5},{5,6},{6,7},{7,8},{8,9},{9,10},{10,1... | collective-permute-start | bytes 157832 | tf_op jit(solution)/shard_map/ppermute | solution.py:14
  579.0 8.3 %collective-permute-start.8 = (f32[1,32,411]{2,1,0:T(8,128)S(1)}, f32[1,32,411]{2,1,0:T(8,128)S(1)}, u32[]{:S(2)}, u32[]{:S(2)}) collective-permute-start(f32[1,32,411]{2,1,0:T(8,128)S(1)} %get-tuple-element.12), channel_id=1, source_target_pairs={{1,0},{2,1},{3,2},{4,3},{5,4},{6,5},{7,6},{8,7},{9,8},{10,9},{11,1... | collective-permute-start | bytes 157832 | tf_op jit(solution)/shard_map/ppermute | solution.py:15
  587.3 1.4 collective-permute-start.10
  587.3 4.3 collective-permute-start.11
Sparse Core Ops, SparseCore 0:
  75.2 47.6 all-gather.3
  125.9 66.5 all-gather.5
  194.7 73.6 all-gather.7
  275.7 118.6 all-reduce.2
  397.4 115.9 all-reduce.4
where the time goes:
time: 600 us; the launch traced here: 599 us
  waiting for transfers between devices  470 us (78%)
  blocking collectives  61.6 us (10%)
  starting transfers between devices  33 us (6%)
  between operations  13.5 us (2%)
  matrix products  12.8 us (2%)
    psum x1, waiting for transfers between devices, body(): lax.psum(lax.dot_general(weights, cotangent, (((1,), (1,)), ((), ())), pr...  119 us
    psum x1, waiting for transfers between devices, body(): summed_grad = lax.psum(part_grad, 'chan')  117 us
    all_gather x1, waiting for transfers between devices, body(): lax.all_gather(inv_cov, 'tile', axis=0, tiled=True)  75.9 us
    all_gather x1, waiting for transfers between devices, body(): all_depart = lax.all_gather(departure, 'chan', axis=1, tiled=True)  66.2 us
    all_gather x1, waiting for transfers between devices, body(): lax.all_gather(active, 'chan', axis=0, tiled=True)  47.4 us
    all_to_all x1, blocking collectives, body(): lax.all_to_all(outgoing.astype(jnp.bfloat16), 'tile', split_axis=0, conca...  35.1 us
    all_gather x1, blocking collectives, body(): lax.all_gather(columns, 'chan', axis=0, tiled=True)  26.5 us
    all_to_all x1, waiting for transfers between devices, body(): lax.all_to_all(summed_grad, 'tile', split_axis=0, concat_axis=0, tiled=True)  21.3 us
  transfers between devices with their start and end apart: 18, of which 15 were waited for; matrix products, arithmetic and copies ran while one was open for 0% of the time, Pallas kernels for 0%

commit v1 on v0

--- a/solution.py
+++ b/solution.py
@@ -110,7 +110,7 @@
     part_grad = lax.dot_general(
         grad_pre, w_hidden, (((0,), (1,)), ((), ())), preferred_element_type=jnp.float32
     )
-    summed_grad = lax.psum(part_grad, "chan")
+    summed_grad = jax.lax.all_gather(part_grad, "chan").sum(axis=0)
     returned = lax.all_to_all(summed_grad, "tile", split_axis=0, concat_axis=0, tiled=True)
     own_slots = lax.dynamic_slice_in_dim(slot_of, chan_index * own_cols, own_cols, 0)
     column_grad = jnp.take(returned, own_slots, axis=0)

time: 600 us -> 576 us (0.960)
  waiting for transfers between devices: 470 us -> 438 us
  local copies, waits for them, and re-layouts: 2.51 us -> 9.52 us
    psum x1 -> x0, waiting for transfers between devices: 117 us -> none  [body(): summed_grad = lax.psum(part_grad, 'chan')]
    all_gather x0 -> x1, waiting for transfers between devices: none -> 85.3 us  [body(): summed_grad = jax.lax.all_gather(part_grad, 'chan').sum(axis=0)]
    unnamed x14 -> x15, local copies, waits for them, and re-layouts: 0.03 us -> 6.04 us
where the time goes in v1:
time: 576 us
  waiting for transfers between devices  438 us (76%)
  blocking collectives  61.6 us (11%)
  starting transfers between devices  33.2 us (6%)
  between operations  13.5 us (2%)
  matrix products  12.8 us (2%)
  local copies, waits for them, and re-layouts  9.52 us (2%)
  other arithmetic  7.14 us (1%)
    psum x1, waiting for transfers between devices, body(): lax.psum(lax.dot_general(weights, cotangent, (((1,), (1,)), ((), ())), pr...  119 us
    all_gather x1, waiting for transfers between devices, body(): summed_grad = jax.lax.all_gather(part_grad, 'chan').sum(axis=0)  85.3 us
    all_gather x1, waiting for transfers between devices, body(): lax.all_gather(inv_cov, 'tile', axis=0, tiled=True)  75.9 us
    all_gather x1, waiting for transfers between devices, body(): all_depart = lax.all_gather(departure, 'chan', axis=1, tiled=True)  66.2 us
    all_gather x1, waiting for transfers between devices, body(): lax.all_gather(active, 'chan', axis=0, tiled=True)  47.4 us
    all_to_all x1, blocking collectives, body(): lax.all_to_all(outgoing.astype(jnp.bfloat16), 'tile', split_axis=0, conca...  35.1 us
    all_gather x1, blocking collectives, body(): lax.all_gather(columns, 'chan', axis=0, tiled=True)  26.5 us
    all_to_all x1, waiting for transfers between devices, body(): lax.all_to_all(summed_grad, 'tile', split_axis=0, concat_axis=0, tiled=True)  21.3 us
  transfers between devices with their start and end apart: 18, of which 15 were waited for; matrix products, arithmetic and copies ran while one was open for 0% of the time, Pallas kernels for 0%

profile of v1, /device:TPU:6, one launch (start us, length us, event | category | flops | bytes accessed | tf_op | source)
XLA Modules:
  0.0 575.6 jit_solution(11115896413589544427)
XLA Ops:
  6.6 0.9 copy.24
  7.5 1.0 reduce_sum.44
  8.6 3.3 convert_reduce_fusion
  12.0 26.5 %all_gather.18 = bf16[128,411]{1,0:T(8,128)(2,1)S(1)} all-gather(bf16[8,411]{1,0:T(8,128)(2,1)S(1)} %multiply_convert_fusion.3), channel_id=1, replica_groups=mesh['tile'=32,'chan'=16] {'chan'}, dimensions={0}, use_global_device_ids=true | all-gather | bytes 111792 | tf_op jit(solution)/shard_map/all_gather | solution.py:70
  38.5 0.2 dynamic-slice_reduce_fusion
  38.6 0.3 convolution_convert_fusion
  38.9 0.1 copy.27
  39.1 35.1 %all_to_all.24 = bf16[32,8,411]{2,1,0:T(8,128)(2,1)S(1)} all-to-all(bf16[32,8,411]{2,1,0:T(8,128)(2,1)S(1)} %bitcast.33), channel_id=1, replica_groups=mesh['tile'=32,'chan'=16] {'tile'}, dimensions={0} | all-to-all | bytes 420864 | tf_op jit(solution)/shard_map/all_to_all | solution.py:73
  74.2 0.9 multiply_convert_fusion.1
  75.1 0.2 dynamic-slice_reduce_fusion.1
  75.4 0.1 lt.53
  75.5 47.4 %all-gather.6.cloned.1.call-done = bf16[2048,256]{0,1:T(8,128)(2,1)} async-done(((bf16[128,256]{0,1:T(8,128)(2,1)}), bf16[2048,256]{0,1:T(8,128)(2,1)}) %all-gather.6.cloned.1.call-update) | async-done | bytes 1048592 | tf_op jit(solution)/shard_map/all_gather | solution.py:84
  122.9 2.6 fusion.6
  125.6 0.7 all-gather.10.cloned.1.call-update
  126.3 66.2 %all-gather.8.cloned.1.call-done = bf16[256,6144]{1,0:T(8,128)(2,1)} async-done(((bf16[256,384]{1,0:T(8,128)(2,1)}), bf16[256,6144]{1,0:T(8,128)(2,1)}) %all-gather.8.cloned.1.call-update) | async-done | bytes 3145744 | tf_op jit(solution)/shard_map/all_gather | solution.py:92
  192.5 75.9 %all-gather.10.cloned.1.call-done = bf16[6144,384]{1,0:T(8,128)(2,1)} async-done(((bf16[192,384]{1,0:T(8,128)(2,1)}), bf16[6144,384]{1,0:T(8,128)(2,1)}) %all-gather.10.cloned.1.call-update) | async-done | bytes 4718608 | tf_op jit(solution)/shard_map/all_gather | solution.py:96
  268.4 7.1 %convolution_bitcast_fusion = f32[2048,256]{0,1:T(8,128)} fusion(bf16[2048,384]{1,0:T(8,128)(2,1)S(1)} %copy-done, bf16[256,6144]{1,0:T(8,128)(2,1)} %all-gather.8.cloned.1.call-done, bf16[6144,384]{1,0:T(8,128)(2,1)} %all-gather.10.cloned.1.call-done), kind=kOutput, calls=%fused_computation.6 | convolution fusion | flops 1610711040 | bytes 11534336 | tf_op jit(solution)/shard_map/dot_general | solution.py:102
  275.5 0.2 all-gather.12.cloned.1.call-start
  275.8 118.6 %all-reduce.2.cloned.1.call-done = f32[2048,256]{0,1:T(8,128)} async-done(((f32[2048,256]{0,1:T(8,128)}), f32[2048,256]{0,1:T(8,128)}) %all-reduce.2.cloned.1.call-update) | async-done | bytes 2097168 | tf_op jit(solution)/shard_map/psum | solution.py:101
  394.4 1.9 fusion.34
  396.3 85.3 %all-gather.12.cloned.1.call-done = f32[4096,411]{0,1:T(8,128)} async-done(((f32[256,411]{0,1:T(8,128)}), f32[4096,411]{0,1:T(8,128)}) %all-gather.12.cloned.1.call-update) | async-done | bytes 6733840 | tf_op jit(solution)/shard_map/all_gather | solution.py:113
  481.6 6.0 %copy.30 = f32[52,8,16,256]{3,2,1,0:T(8,128)S(1)} copy(f32[52,8,16,256]{3,1,2,0:T(8,128)} %bitcast.32) | data formatting | bytes 13631488
  487.7 1.2 bitcast_reduce_fusion
  488.9 1.0 copy.28
  489.9 12.6 %all-to-all-start.1 = ((f32[32,8,411]{2,1,0:T(8,128)}), f32[32,8,411]{2,1,0:T(8,128)S(1)}, u32[]{:S(2)}, u32[]{:S(2)}) async-start(f32[32,8,411]{2,1,0:T(8,128)} %bitcast.5), calls=%async_computation.1 | async-start | bytes 1048576 | tf_op jit(solution)/shard_map/all_to_all | solution.py:114
  502.5 3.4 collective-permute-start.2
  505.9 2.5 collective-permute-start
  508.4 0.2 dynamic-slice_reduce_fusion.2
  508.6 4.8 collective-permute-done
  513.6 1.7 collective-permute-start.4
  515.2 21.3 %all-to-all-done.1 = f32[32,8,411]{2,1,0:T(8,128)S(1)} async-done(((f32[32,8,411]{2,1,0:T(8,128)}), f32[32,8,411]{2,1,0:T(8,128)S(1)}, u32[]{:S(2)}, u32[]{:S(2)}) %all-to-all-start.1) | async-done | bytes 420896 | tf_op jit(solution)/shard_map/all_to_all | solution.py:114
  536.5 0.6 gather_fusion
  537.2 3.4 collective-permute-start.3
  540.6 2.5 collective-permute-start.1
  543.2 0.2 collective-permute-done.3
  543.4 5.5 collective-permute-done.1
  548.9 0.5 collective-permute-start.7
  549.5 0.8 collective-permute-done.5
  550.3 2.9 collective-permute-done.7
  553.3 0.2 fusion.23
  553.5 1.9 collective-permute-start.9
  555.5 3.9 collective-permute-start.8
  559.4 0.3 collective-permute-done.9
  559.7 4.0 collective-permute-done.8
  563.8 0.5 collective-permute-start.11
  564.3 0.9 collective-permute-done.10
  565.2 2.9 collective-permute-done.11
  568.1 0.9 fusion.11
  (52 shorter events, 0.9 us)
Async XLA Ops:
  6.5 116.4 %copy-start = (bf16[2048,384]{1,0:T(8,128)(2,1)S(1)}, bf16[2048,384]{1,0:T(8,128)(2,1)}, u32[]{:S(2)}) copy-start(bf16[2048,384]{1,0:T(8,128)(2,1)} %param.17) | copy-start | bytes 4718596
  6.5 67.7 %copy-start.1 = (bf16[411,128]{1,0:T(8,128)(2,1)S(1)}, bf16[411,128]{1,0:T(8,128)(2,1)}, u32[]{:S(2)}) copy-start(bf16[411,128]{1,0:T(8,128)(2,1)} %param.15) | copy-start | bytes 315652
  6.5 67.7 %copy-start.6 = (f32[128]{0:T(128)S(1)}, f32[128]{0:T(128)}, u32[]{:S(2)}) copy-start(f32[128]{0:T(128)} %param.16) | copy-start | bytes 1540
  6.5 69.0 %copy-start.3 = (s32[256]{0:T(256)S(1)}, s32[256]{0:T(256)}, u32[]{:S(2)}) copy-start(s32[256]{0:T(256)} %param.14) | copy-start | bytes 3076
  6.5 116.4 %copy-start.5 = (f32[384]{0:T(512)S(1)}, f32[384]{0:T(512)}, u32[]{:S(2)}) copy-start(f32[384]{0:T(512)} %param.18) | copy-start | bytes 4612
  6.5 116.4 %copy-start.4 = (bf16[256,384]{1,0:T(8,128)(2,1)S(1)}, bf16[256,384]{1,0:T(8,128)(2,1)}, u32[]{:S(2)}) copy-start(bf16[256,384]{1,0:T(8,128)(2,1)} %param.13) | copy-start | bytes 589828
  6.6 116.4 %all-gather.6.cloned.1.call-start = ((), (), s32[]{:S(2)}) async-start(), calls=%async_computation.2 | async-start | bytes 1114112 | tf_op jit(solution)/shard_map/all_gather | solution.py:84
  75.1 117.4 %all-gather.8.cloned.1.call-start = ((), (), s32[]{:S(2)}) async-start(), calls=%async_computation.3 | async-start | bytes 3342336 | tf_op jit(solution)/shard_map/all_gather | solution.py:92
  125.6 142.8 %all-gather.10.cloned.1.call-start = ((), (), s32[]{:S(2)}) async-start(), calls=%async_computation.4 | async-start | bytes 4866048 | tf_op jit(solution)/shard_map/all_gather | solution.py:96
  126.3 268.1 %all-reduce.2.cloned.1.call-start = ((), (), s32[]{:S(2)}) async-start(), calls=%async_computation.5 | async-start | bytes 4194304 | tf_op jit(solution)/shard_map/psum | solution.py:101
  275.5 206.1 %all-gather.12.cloned.1.call-start = ((), (), s32[]{:S(2)}) async-start(), calls=%async_computation.6 | async-start | bytes 7241728 | tf_op jit(solution)/shard_map/all_gather | solution.py:113
  487.6 14.9 %copy-start.2 = (f32[4,32]{1,0:T(4,128)S(1)}, f32[4,32]{1,0:T(4,128)}, u32[]{:S(2)}) copy-start(f32[4,32]{1,0:T(4,128)} %param.11) | copy-start | bytes 1540
  489.9 46.6 %all-to-all-start.1 = ((f32[32,8,411]{2,1,0:T(8,128)}), f32[32,8,411]{2,1,0:T(8,128)S(1)}, u32[]{:S(2)}, u32[]{:S(2)}) async-start(f32[32,8,411]{2,1,0:T(8,128)} %bitcast.5), calls=%async_computation.1 | async-start | bytes 1048576 | tf_op jit(solution)/shard_map/all_to_all | solution.py:114
  502.5 6.1 %collective-permute-start.2 = (f32[1,32]{1,0:T(1,128)S(1)}, f32[1,32]{1,0:T(1,128)S(1)}, u32[]{:S(2)}, u32[]{:S(2)}) collective-permute-start(f32[1,32]{1,0:T(1,128)S(1)} %get-tuple-element.23), channel_id=1, source_target_pairs={{0,1},{1,2},{2,3},{3,4},{4,5},{5,6},{6,7},{7,8},{8,9},{9,10},{10,1... | collective-permute-start | bytes 392 | tf_op jit(solution)/shard_map/ppermute | solution.py:14
  505.9 7.6 %collective-permute-start = (f32[1,32]{1,0:T(1,128)S(1)}, f32[1,32]{1,0:T(1,128)S(1)}, u32[]{:S(2)}, u32[]{:S(2)}) collective-permute-start(f32[1,32]{1,0:T(1,128)S(1)} %get-tuple-element.24), channel_id=1, source_target_pairs={{1,0},{2,1},{3,2},{4,3},{5,4},{6,5},{7,6},{8,7},{9,8},{10,9},{11,1... | collective-permute-start | bytes 392 | tf_op jit(solution)/shard_map/ppermute | solution.py:15
  513.6 29.5 %collective-permute-start.4 = (f32[6,1]{1,0:T(8,128)S(1)}, f32[6,1]{1,0:T(8,128)S(1)}, u32[]{:S(2)}, u32[]{:S(2)}) collective-permute-start(f32[6,1]{1,0:T(8,128)S(1)} %get-tuple-element.13), channel_id=1, source_target_pairs={{16,0},{32,16},{48,32},{64,48},{80,64},{96,80},{112,96},{128,112},... | collective-permute-start | bytes 80 | tf_op jit(solution)/shard_map/ppermute | solution.py:15
  515.2 27.8 %collective-permute-start.6 = (f32[6,1]{1,0:T(8,128)S(1)}, f32[6,1]{1,0:T(8,128)S(1)}, u32[]{:S(2)}, u32[]{:S(2)}) collective-permute-start(f32[6,1]{1,0:T(8,128)S(1)} %get-tuple-element.14), channel_id=1, source_target_pairs={{0,16},{16,32},{32,48},{48,64},{64,80},{80,96},{96,112},{112,128},... | collective-permute-start | bytes 80 | tf_op jit(solution)/shard_map/ppermute | solution.py:14
  537.2 6.2 %collective-permute-start.3 = (f32[1,32,411]{2,1,0:T(8,128)S(1)}, f32[1,32,411]{2,1,0:T(8,128)S(1)}, u32[]{:S(2)}, u32[]{:S(2)}) collective-permute-start(f32[1,32,411]{2,1,0:T(8,128)S(1)} %mul.151), channel_id=1, source_target_pairs={{0,1},{1,2},{2,3},{3,4},{4,5},{5,6},{6,7},{7,8},{8,9},{9,10},{10,1... | collective-permute-start | bytes 157832 | tf_op jit(solution)/shard_map/ppermute | solution.py:14
  540.6 8.3 %collective-permute-start.1 = (f32[1,32,411]{2,1,0:T(8,128)S(1)}, f32[1,32,411]{2,1,0:T(8,128)S(1)}, u32[]{:S(2)}, u32[]{:S(2)}) collective-permute-start(f32[1,32,411]{2,1,0:T(8,128)S(1)} %mul.151), channel_id=1, source_target_pairs={{1,0},{2,1},{3,2},{4,3},{5,4},{6,5},{7,6},{8,7},{9,8},{10,9},{11,1... | collective-permute-start | bytes 157832 | tf_op jit(solution)/shard_map/ppermute | solution.py:15
  548.9 1.4 collective-permute-start.5
  548.9 4.3 collective-permute-start.7
  553.5 6.2 %collective-permute-start.9 = (f32[1,32,411]{2,1,0:T(8,128)S(1)}, f32[1,32,411]{2,1,0:T(8,128)S(1)}, u32[]{:S(2)}, u32[]{:S(2)}) collective-permute-start(f32[1,32,411]{2,1,0:T(8,128)S(1)} %get-tuple-element.11), channel_id=1, source_target_pairs={{0,1},{1,2},{2,3},{3,4},{4,5},{5,6},{6,7},{7,8},{8,9},{9,10},{10,1... | collective-permute-start | bytes 157832 | tf_op jit(solution)/shard_map/ppermute | solution.py:14
  555.5 8.3 %collective-permute-start.8 = (f32[1,32,411]{2,1,0:T(8,128)S(1)}, f32[1,32,411]{2,1,0:T(8,128)S(1)}, u32[]{:S(2)}, u32[]{:S(2)}) collective-permute-start(f32[1,32,411]{2,1,0:T(8,128)S(1)} %get-tuple-element.12), channel_id=1, source_target_pairs={{1,0},{2,1},{3,2},{4,3},{5,4},{6,5},{7,6},{8,7},{9,8},{10,9},{11,1... | collective-permute-start | bytes 157832 | tf_op jit(solution)/shard_map/ppermute | solution.py:15
  563.7 1.4 collective-permute-start.10
  563.8 4.3 collective-permute-start.11
Sparse Core Ops, SparseCore 0:
  75.2 47.6 all-gather.5
  125.9 66.5 all-gather.7
  194.7 73.6 all-gather.9
  275.7 118.6 all-reduce.1
  397.2 84.3 all-gather.11
